TPU v7x, 256 devices: a whole 4x4x8 slice. The times are simulated.
256 devices in a mesh: ctx: 16 (over y, x), exp: 16 (over z, core).
Axes of the slice: x: 4, y: 4, z: 8, core: 2. Of those that a mesh axis runs over, the one named last changes fastest.
Arguments:
- tokens: bfloat16 [2048, 4096], P('ctx', 'exp'), may hold values from -6 to 6
- input_weight: bfloat16 [4096, 8192], P('ctx', 'exp'), may hold values from -0.09375 to 0.09375
- gate_weight: bfloat16 [4096, 8192], P('ctx', 'exp'), may hold values from -0.09375 to 0.09375
- conv_weight: float32 [4, 8192], P(None, 'exp'), may hold values from -3 to 3
- conv_bias: float32 [8192], P('exp'), may hold values from -3 to 3
- state_weight: bfloat16 [8192, 32], P('exp'), may hold values from -0.0078125 to 0.0078125
- step_size: float32 [2048, 8192], P('ctx', 'exp'), may hold values from 0 to 1, as said below
- skip_gain: float32 [8192], P('exp'), may hold values from 0.5 to 2
- output_weight: bfloat16 [8192, 4096], P('exp', 'ctx'), may hold values from -0.0625 to 0.0625
- norm_gain: float32 [4096], replicated, may hold values from 0.1 to 1.9
- router_weight: bfloat16 [4096, 16], replicated, may hold values from -0.09375 to 0.09375
- expert_gate: bfloat16 [16, 7168, 4096], P('exp', 'ctx'), may hold values from -0.09375 to 0.09375
- expert_up: bfloat16 [16, 7168, 4096], P('exp', 'ctx'), may hold values from -0.09375 to 0.09375
- expert_down: bfloat16 [16, 7168, 4096], P('exp', 'ctx'), may hold values from -0.0625 to 0.0625
- expert_ids: int32 [2048, 2], P(('ctx', 'exp')), may hold values from 0 to 15, all different within a row; in each aligned block of 8 rows (0 to 7, 8 to 15, ...) at most 2 rows name the same one
Outputs:
- layer_out: bfloat16 [2048, 4096], P(('ctx', 'exp'))
Inputs may be any that keep to these rules, and one draw needn't show every extreme that they name: `expert_ids`: each token names 2 different experts; in each aligned block of 8 tokens no expert is named by more than 2 tokens. `step_size`: a positive rate for each token and channel.
All inputs are finite; a program needn't handle non-finite values.
Results may differ from a plain program's by a relative error of at most 0.028.
Values may be sent and summed in bfloat16 or wider, within the bound.
A program may use at most 128 MiB of HBM per device.

v0:
```python
import jax
import jax.numpy as jnp
from jax import lax
from jax.sharding import PartitionSpec as P

STATE = 16
CONV = 4
TOP = 2
CAP = 2
precise = lax.Precision.HIGHEST


def shifted(shard, axis, by):
    devices = lax.axis_size(axis)
    pairs = [(i, i + by) for i in range(devices) if 0 <= i + by < devices]
    return lax.ppermute(shard, axis, pairs)


def causal_part(scores, decay_block, input_block):
    length = decay_block.shape[0]
    causal = (jnp.arange(length)[:, None] >= jnp.arange(length)[None, :])[:, :, None]
    distance = decay_block[:, None, :] - decay_block[None, :, :]
    weight = jnp.where(causal, jnp.exp(-jnp.where(causal, distance, 0.0)), 0.0)
    return jnp.einsum("ts,tsc,sc->tc", scores, weight, input_block, precision=precise)


def local(
    tokens,
    input_weight,
    gate_weight,
    conv_weight,
    conv_bias,
    state_weight,
    step_size,
    skip_gain,
    output_weight,
    norm_gain,
    router_weight,
    expert_gate,
    expert_up,
    expert_down,
    expert_ids,
):
    whole_stretch = lax.all_gather(tokens, "exp", axis=1, tiled=True)
    stretch_rows = whole_stretch.shape[0]
    inner_width = input_weight.shape[1]
    inner_x = jnp.dot(
        whole_stretch,
        lax.all_gather(input_weight, "ctx", axis=0, tiled=True),
        preferred_element_type=jnp.float32,
    )
    inner_z = jnp.dot(
        whole_stretch,
        lax.all_gather(gate_weight, "ctx", axis=0, tiled=True),
        preferred_element_type=jnp.float32,
    )
    inner_x = inner_x.astype(jnp.bfloat16)
    inner_z = inner_z.astype(jnp.bfloat16)
    earlier_rows = shifted(inner_x[stretch_rows - (CONV - 1) :], "ctx", 1)
    extended = jnp.concatenate([earlier_rows, inner_x], 0).astype(jnp.float32)
    filtered = jnp.broadcast_to(conv_bias[None, :], (stretch_rows, inner_width))
    for offset in range(CONV):
        filtered = (
            filtered + conv_weight[offset][None, :] * extended[offset : offset + stretch_rows]
        )
    mixer_in = jax.nn.silu(filtered).astype(jnp.bfloat16)
    mixer_wide = mixer_in.astype(jnp.float32)
    projections = lax.psum(
        jnp.dot(mixer_in, state_weight, preferred_element_type=jnp.float32), "exp"
    )
    input_gain = projections[:, :STATE]
    readout = projections[:, STATE:]
    cumulative = jnp.cumsum(step_size, 0)
    scores = jnp.dot(readout, input_gain.T, precision=precise)
    block_width = 128
    block_count = inner_width // block_width
    decay_blocks = cumulative.reshape(stretch_rows, block_count, block_width).transpose(1, 0, 2)
    incoming_slabs = mixer_wide.reshape(stretch_rows, block_count, block_width).transpose(1, 0, 2)
    inside = lax.map(
        lambda paired: causal_part(scores, paired[0], paired[1]), (decay_blocks, incoming_slabs)
    )
    inside = inside.transpose(1, 0, 2).reshape(stretch_rows, inner_width)
    total_decay = cumulative[stretch_rows - 1]
    tail_weight = jnp.exp(-(total_decay[None, :] - cumulative)) * mixer_wide
    local_end = jnp.dot(tail_weight.T, input_gain, precision=precise)
    stretch_keep = jnp.exp(-total_decay)

    def relay_step(turn_index, received):
        leaving = stretch_keep[:, None] * received + local_end
        return shifted(leaving, "ctx", 1)

    entering = lax.fori_loop(0, lax.axis_size("ctx") - 1, relay_step, jnp.zeros_like(local_end))
    carried = jnp.exp(-cumulative) * jnp.dot(readout, entering.T, precision=precise)
    mixed_state = (inside + carried + skip_gain[None, :] * mixer_wide) * jax.nn.silu(
        inner_z.astype(jnp.float32)
    )
    blender_result = mixed_state.astype(jnp.bfloat16)
    row_count = expert_ids.shape[0]
    start_row = lax.axis_index("exp") * row_count
    own_tokens = lax.dynamic_slice_in_dim(whole_stretch, start_row, row_count, 0)
    out_whole = lax.all_gather(output_weight, "ctx", axis=1, tiled=True)
    projected = lax.psum_scatter(
        jnp.dot(blender_result, out_whole, preferred_element_type=jnp.float32).astype(jnp.bfloat16),
        "exp",
        scatter_dimension=0,
        tiled=True,
    ).astype(jnp.float32)
    residual = (own_tokens.astype(jnp.float32) + projected).astype(jnp.bfloat16)
    stream = residual.astype(jnp.float32)
    normed = (
        stream
        * lax.rsqrt(jnp.mean(stream * stream, -1, keepdims=True) + 1e-05)
        * norm_gain[None, :]
    ).astype(jnp.bfloat16)
    logits = jnp.dot(normed, router_weight, preferred_element_type=jnp.float32)
    experts = router_weight.shape[1]
    expert_range = jnp.arange(experts, dtype=jnp.int32)
    chosen = expert_ids[:, :, None] == expert_range[None, None, :]
    selected_entry = jnp.sum(jnp.where(chosen, logits[:, None, :], 0.0), -1)
    shares = jax.nn.sigmoid(selected_entry - selected_entry[:, ::-1])
    flat_hits = chosen.reshape(row_count * TOP, experts).astype(jnp.int32)
    earlier_hits = jnp.cumsum(flat_hits, 0) - flat_hits
    slot_index = jnp.sum(earlier_hits * flat_hits, -1)
    target = expert_ids.reshape(-1) * CAP + slot_index
    placed = target[:, None] == jnp.arange(experts * CAP, dtype=jnp.int32)[None, :]
    placed = placed.reshape(row_count, TOP, experts * CAP)
    selector = jnp.any(placed, 1).astype(jnp.bfloat16)
    outgoing = lax.dot_general(
        selector, normed, (((0,), (0,)), ((), ())), preferred_element_type=jnp.float32
    ).astype(jnp.bfloat16)
    outgoing = outgoing.reshape(experts, CAP, -1)
    arrived = lax.all_to_all(outgoing, "exp", split_axis=0, concat_axis=0, tiled=True)
    arrived = arrived.reshape(-1, arrived.shape[2])
    gate_part = expert_gate[0]
    up_part = expert_up[0]
    down_part = expert_down[0]
    shard_rows = lax.all_gather(arrived, "ctx", axis=0, tiled=True)
    gate_value = lax.dot_general(
        shard_rows, gate_part, (((1,), (1,)), ((), ())), preferred_element_type=jnp.float32
    )
    up_value = lax.dot_general(
        shard_rows, up_part, (((1,), (1,)), ((), ())), preferred_element_type=jnp.float32
    )
    hidden = (jax.nn.silu(gate_value) * up_value).astype(jnp.bfloat16)
    partial_out = jnp.dot(hidden, down_part, preferred_element_type=jnp.float32)
    finished = lax.psum_scatter(
        partial_out.astype(jnp.bfloat16), "ctx", scatter_dimension=0, tiled=True
    )
    returned = lax.all_to_all(
        finished.reshape(experts, CAP, -1), "exp", split_axis=0, concat_axis=0, tiled=True
    )
    returned = returned.reshape(experts * CAP, -1).astype(jnp.float32)
    combine = jnp.sum(jnp.where(placed, shares[:, :, None], 0.0), 1)
    moe_out = jnp.dot(combine, returned, precision=precise)
    return (stream + moe_out).astype(jnp.bfloat16)


def solution(mesh):
    in_specs = (
        P("ctx", "exp"),
        P("ctx", "exp"),
        P("ctx", "exp"),
        P(None, "exp"),
        P("exp"),
        P("exp", None),
        P("ctx", "exp"),
        P("exp"),
        P("exp", "ctx"),
        P(),
        P(),
        P("exp", "ctx", None),
        P("exp", "ctx", None),
        P("exp", "ctx", None),
        P(("ctx", "exp"), None),
    )
    out_specs = P(("ctx", "exp"), None)
    return jax.shard_map(local, mesh=mesh, in_specs=in_specs, out_specs=out_specs, check_vma=False)
```

profile of v0, /device:TPU:1, one launch (start us, length us, event | category | flops | bytes accessed | tf_op | source)
XLA Modules:
  0.0 636.4 jit_solution(2759990935749958650)
XLA Ops:
  11.5 39.5 %all-gather.6.cloned.1.call-done = bf16[128,4096]{1,0:T(8,128)(2,1)} async-done(((bf16[128,256]{1,0:T(8,128)(2,1)}), bf16[128,4096]{1,0:T(8,128)(2,1)}) %all-gather.6.cloned.1.call-update) | async-done | bytes 1048592 | tf_op jit(solution)/shard_map/all_gather | solution.py:44
  51.0 57.7 %all-gather.8.cloned.1.call-done = bf16[4096,512]{1,0:T(8,128)(2,1)} async-done(((bf16[256,512]{1,0:T(8,128)(2,1)}), bf16[4096,512]{1,0:T(8,128)(2,1)}) %all-gather.8.cloned.1.call-update) | async-done | bytes 4194320 | tf_op jit(solution)/shard_map/all_gather | solution.py:49
  115.1 52.4 %all-gather.10.cloned.1.call-done = bf16[4096,512]{1,0:T(8,128)(2,1)} async-done(((bf16[256,512]{1,0:T(8,128)(2,1)}), bf16[4096,512]{1,0:T(8,128)(2,1)}) %all-gather.10.cloned.1.call-update) | async-done | bytes 4194320 | tf_op jit(solution)/shard_map/all_gather | solution.py:54
  170.7 46.7 %psum.7 = f32[128,32]{0,1:T(8,128)S(1)} all-reduce(f32[128,32]{0,1:T(8,128)S(1)} %fusion.54), channel_id=1, replica_groups=mesh['ctx'=16,'exp'=16] {'exp'}, use_global_device_ids=true, to_apply=%region_1.2 | all-reduce | flops 4096 | bytes 32768 | tf_op jit(solution)/shard_map/psum | solution.py:68
  218.1 39.1 %while.20 = (s32[]{:T(128)}, f32[4,128,128]{2,1,0:T(8,128)S(1)}, f32[4,128,128]{2,1,0:T(8,128)S(1)}, f32[4,128,128]{2,1,0:T(8,128)S(1)}, f32[128,128]{1,0:T(8,128)S(1)}, /*index=5*/s32[]{:T(128)}) while((s32[]{:T(128)}, f32[4,128,128]{2,1,0:T(8,128)S(1)}, f32[4,128,128]{2,1,0:T(8,128)S(1)}, f32[4,128,128]{2,1,0:T(8,128)S(1)}, ...), condition=%wide.region_3.4_spmd, body=%wide.region_2.3_spmd.sunk | while | flops 35667968 | bytes 688205 | solution.py:79
  218.1 9.7 %fusion.87 = f32[128,1,128]{2,1,0:T(1,128)S(1)} fusion(f32[128,128,1]{1,2,0:T(1,128)S(1)} %bitcast.88, f32[128,128]{1,0:T(8,128)S(1)} %get-tuple-element.140, f32[128,128]{1,0:T(8,128)S(1)} %get-tuple-element.141, pred[128,128]{1,0:T(8,128)(4,1)S(1)} %iota_compare_fusion.5), kind=kOutput, calls=%fused_computation.clone.1 | convolution fusion | flops 35651584 | bytes 278528 | tf_op jit(solution)/shard_map/while/body/eval_jaxpr/ts,tsc,sc->tc/dot_general | solution.py:24
  227.9 9.7 %fusion.87 = f32[128,1,128]{2,1,0:T(1,128)S(1)} fusion(f32[128,128,1]{1,2,0:T(1,128)S(1)} %bitcast.88, f32[128,128]{1,0:T(8,128)S(1)} %get-tuple-element.140, f32[128,128]{1,0:T(8,128)S(1)} %get-tuple-element.141, pred[128,128]{1,0:T(8,128)(4,1)S(1)} %iota_compare_fusion.5), kind=kOutput, calls=%fused_computation.clone.1 | convolution fusion | flops 35651584 | bytes 278528 | tf_op jit(solution)/shard_map/while/body/eval_jaxpr/ts,tsc,sc->tc/dot_general | solution.py:24
  237.6 9.7 %fusion.87 = f32[128,1,128]{2,1,0:T(1,128)S(1)} fusion(f32[128,128,1]{1,2,0:T(1,128)S(1)} %bitcast.88, f32[128,128]{1,0:T(8,128)S(1)} %get-tuple-element.140, f32[128,128]{1,0:T(8,128)S(1)} %get-tuple-element.141, pred[128,128]{1,0:T(8,128)(4,1)S(1)} %iota_compare_fusion.5), kind=kOutput, calls=%fused_computation.clone.1 | convolution fusion | flops 35651584 | bytes 278528 | tf_op jit(solution)/shard_map/while/body/eval_jaxpr/ts,tsc,sc->tc/dot_general | solution.py:24
  247.4 9.7 %fusion.87 = f32[128,1,128]{2,1,0:T(1,128)S(1)} fusion(f32[128,128,1]{1,2,0:T(1,128)S(1)} %bitcast.88, f32[128,128]{1,0:T(8,128)S(1)} %get-tuple-element.140, f32[128,128]{1,0:T(8,128)S(1)} %get-tuple-element.141, pred[128,128]{1,0:T(8,128)(4,1)S(1)} %iota_compare_fusion.5), kind=kOutput, calls=%fused_computation.clone.1 | convolution fusion | flops 35651584 | bytes 278528 | tf_op jit(solution)/shard_map/while/body/eval_jaxpr/ts,tsc,sc->tc/dot_general | solution.py:24
  257.1 90.6 %while.21 = (s32[]{:T(128)}, f32[512,16]{0,1:T(8,128)S(1)}, f32[512]{0:T(512)S(1)}, f32[512,16]{0,1:T(8,128)S(1)}, s32[]{:T(128)}) while((s32[]{:T(128)}, f32[512,16]{0,1:T(8,128)S(1)}, f32[512]{0:T(512)S(1)}, f32[512,16]{0,1:T(8,128)S(1)}, s32[]{:T(128)}) %tuple.40), condition=%wide.region_5.6_spmd, body=%wide.region_4.5_spmd.sunk | while | flops 16386 | bytes 231525 | solution.py:92
  260.9 3.6 collective-permute-start
  270.2 4.0 collective-permute-start
  275.3 3.7 collective-permute-start
  280.0 5.8 collective-permute-start
  286.8 5.7 collective-permute-start
  293.5 5.8 collective-permute-start
  300.3 5.8 collective-permute-start
  307.1 5.8 collective-permute-start
  313.8 5.8 collective-permute-start
  320.6 5.8 collective-permute-start
  327.6 5.6 collective-permute-start
  334.2 5.8 collective-permute-start
  340.9 5.8 collective-permute-start
  348.2 3.9 convolution_convert_fusion.1
  352.9 81.0 %reduce-scatter.3.cloned.1.call-done = bf16[8,4096]{1,0:T(8,128)(2,1)} async-done(((bf16[128,4096]{1,0:T(8,128)(2,1)}), bf16[8,4096]{1,0:T(8,128)(2,1)}) %reduce-scatter.3.cloned.1.call-update) | async-done | bytes 65552 | tf_op jit(solution)/shard_map/reduce_scatter | solution.py:102
  435.4 19.1 %all_to_all.10 = bf16[16,2,4096]{2,1,0:T(2,128)(2,1)S(1)} all-to-all(bf16[16,2,4096]{2,1,0:T(2,128)(2,1)S(1)} %reshape.74), channel_id=1, replica_groups=mesh['ctx'=16,'exp'=16] {'exp'}, dimensions={0} | all-to-all | bytes 524288 | tf_op jit(solution)/shard_map/all_to_all | solution.py:132
  455.5 53.0 %all-gather.14.cloned.1.call-done = bf16[512,4096]{1,0:T(8,128)(2,1)} async-done(((bf16[32,4096]{1,0:T(8,128)(2,1)}), bf16[512,4096]{1,0:T(8,128)(2,1)}) %all-gather.14.cloned.1.call-update) | async-done | bytes 4194320 | tf_op jit(solution)/shard_map/all_gather | solution.py:137
  508.5 5.4 fusion.18
  513.9 10.8 %convolution_convert_fusion = bf16[512,4096]{1,0:T(8,128)(2,1)} fusion(bf16[1,448,4096]{2,1,0:T(8,128)(2,1)} %param.32, bf16[512,4096]{1,0:T(8,128)(2,1)} %all-gather.14.cloned.1.call-done, bf16[1,448,4096]{2,1,0:T(8,128)(2,1)} %param.31, f32[512,448]{0,1:T(8,128)S(1)} %fusion.18), kind=kOutput, calls=%fused_computation.19 | convolution fusion | flops 3761569792 | bytes 16646144 | tf_op jit(solution)/shard_map/dot_general | solution.py:145
  524.7 81.0 %reduce-scatter.5.cloned.1.call-done = bf16[32,4096]{1,0:T(8,128)(2,1)} async-done(((bf16[512,4096]{1,0:T(8,128)(2,1)}), bf16[32,4096]{1,0:T(8,128)(2,1)}) %reduce-scatter.5.cloned.1.call-update) | async-done | bytes 262160 | tf_op jit(solution)/shard_map/reduce_scatter | solution.py:146
  607.5 9.3 %all-to-all-start.1 = ((bf16[16,2,4096]{2,1,0:T(2,128)(2,1)}), bf16[16,2,4096]{2,1,0:T(2,128)(2,1)S(1)}, u32[]{:S(2)}, u32[]{:S(2)}) async-start(bf16[16,2,4096]{2,1,0:T(2,128)(2,1)} %reshape.76), calls=%async_computation.3 | async-start | bytes 524288 | tf_op jit(solution)/shard_map/all_to_all | solution.py:149
  617.3 11.2 %all-to-all-done.1 = bf16[16,2,4096]{2,1,0:T(2,128)(2,1)S(1)} async-done(((bf16[16,2,4096]{2,1,0:T(2,128)(2,1)}), bf16[16,2,4096]{2,1,0:T(2,128)(2,1)S(1)}, u32[]{:S(2)}, u32[]{:S(2)}) %all-to-all-start.1) | async-done | bytes 262176 | tf_op jit(solution)/shard_map/all_to_all | solution.py:149
  (113 shorter events, 43.9 us)
Async XLA Ops:
  6.5 610.3 %copy-start = (bf16[4096,16]{0,1:T(8,128)(2,1)S(1)}, bf16[4096,16]{0,1:T(8,128)(2,1)}, u32[]{:S(2)}) copy-start(bf16[4096,16]{0,1:T(8,128)(2,1)} %param.29) | copy-start | bytes 393220
  6.5 44.5 %all-gather.6.cloned.1.call-start = ((), (), s32[]{:S(2)}) async-start(), calls=%async_computation.4 | async-start | bytes 1114112 | tf_op jit(solution)/shard_map/all_gather | solution.py:44
  7.3 101.4 %all-gather.8.cloned.1.call-start = ((), (), s32[]{:S(2)}) async-start(), calls=%async_computation.5 | async-start | bytes 4456448 | tf_op jit(solution)/shard_map/all_gather | solution.py:49
  8.0 159.4 %all-gather.10.cloned.1.call-start = ((), (), s32[]{:S(2)}) async-start(), calls=%async_computation.6 | async-start | bytes 4456448 | tf_op jit(solution)/shard_map/all_gather | solution.py:54
  8.7 339.5 %all-gather.12.cloned.1.call-start = ((), (), s32[]{:S(2)}) async-start(), calls=%async_computation.7 | async-start | bytes 4456448 | tf_op jit(solution)/shard_map/all_gather | solution.py:101
  9.3 424.6 %reduce-scatter.3.cloned.1.call-start = ((), (), s32[]{:S(2)}) async-start(), calls=%async_computation.8 | async-start | bytes 1114112 | tf_op jit(solution)/shard_map/reduce_scatter | solution.py:102
  51.0 116.5 %copy-start.1 = (bf16[128,4096]{1,0:T(8,128)(2,1)S(1)}, bf16[128,4096]{1,0:T(8,128)(2,1)}, u32[]{:S(2)}) copy-start(bf16[128,4096]{1,0:T(8,128)(2,1)} %all-gather.6.cloned.1.call-done) | copy-start | bytes 3145732
  111.9 58.5 %copy-start.5 = (f32[512]{0:T(512)S(1)}, f32[512]{0:T(512)}, u32[]{:S(2)}) copy-start(f32[512]{0:T(512)} %param.23) | copy-start | bytes 6148
  111.9 58.7 %copy-start.2 = (bf16[512,32]{0,1:T(8,128)(2,1)S(1)}, bf16[512,32]{0,1:T(8,128)(2,1)}, u32[]{:S(2)}) copy-start(bf16[512,32]{0,1:T(8,128)(2,1)} %param.24) | copy-start | bytes 98308
  112.0 58.4 %collective-permute-start.1 = (bf16[3,512]{1,0:T(4,128)(2,1)S(1)}, bf16[3,512]{1,0:T(4,128)(2,1)S(1)}, u32[]{:S(2)}, u32[]{:S(2)}) collective-permute-start(bf16[3,512]{1,0:T(4,128)(2,1)S(1)} %slice.48), channel_id=1, source_target_pairs={{0,16},{16,32},{32,48},{48,64},{64,80},{80,96},{96,112},{112,128},... | collective-permute-start | bytes 9224 | tf_op jit(solution)/shard_map/ppermute | solution.py:16
  218.1 129.7 %copy-start.6 = (f32[512]{0:T(512)S(1)}, f32[512]{0:T(512)}, u32[]{:S(2)}) copy-start(f32[512]{0:T(512)} %param.26) | copy-start | bytes 6148
  257.2 3.7 collective-permute-start
  260.9 4.7 collective-permute-start
  265.5 4.7 collective-permute-start
  270.2 5.1 collective-permute-start
  275.3 4.7 collective-permute-start
  280.0 6.9 %collective-permute-start = (f32[512,16]{0,1:T(8,128)S(1)}, f32[512,16]{0,1:T(8,128)S(1)}, u32[]{:S(2)}, u32[]{:S(2)}) collective-permute-start(f32[512,16]{0,1:T(8,128)S(1)} %multiply_add_fusion.3), channel_id=1, source_target_pairs={{0,16},{16,32},{32,48},{48,64},{64,80},{80,96},{96,112},{112,128},... | collective-permute-start | bytes 98312 | tf_op jit(solution)/shard_map/while/body/eval_jaxpr/ppermute | solution.py:16
  286.8 6.7 %collective-permute-start = (f32[512,16]{0,1:T(8,128)S(1)}, f32[512,16]{0,1:T(8,128)S(1)}, u32[]{:S(2)}, u32[]{:S(2)}) collective-permute-start(f32[512,16]{0,1:T(8,128)S(1)} %multiply_add_fusion.3), channel_id=1, source_target_pairs={{0,16},{16,32},{32,48},{48,64},{64,80},{80,96},{96,112},{112,128},... | collective-permute-start | bytes 98312 | tf_op jit(solution)/shard_map/while/body/eval_jaxpr/ppermute | solution.py:16
  293.5 6.8 %collective-permute-start = (f32[512,16]{0,1:T(8,128)S(1)}, f32[512,16]{0,1:T(8,128)S(1)}, u32[]{:S(2)}, u32[]{:S(2)}) collective-permute-start(f32[512,16]{0,1:T(8,128)S(1)} %multiply_add_fusion.3), channel_id=1, source_target_pairs={{0,16},{16,32},{32,48},{48,64},{64,80},{80,96},{96,112},{112,128},... | collective-permute-start | bytes 98312 | tf_op jit(solution)/shard_map/while/body/eval_jaxpr/ppermute | solution.py:16
  300.3 6.8 %collective-permute-start = (f32[512,16]{0,1:T(8,128)S(1)}, f32[512,16]{0,1:T(8,128)S(1)}, u32[]{:S(2)}, u32[]{:S(2)}) collective-permute-start(f32[512,16]{0,1:T(8,128)S(1)} %multiply_add_fusion.3), channel_id=1, source_target_pairs={{0,16},{16,32},{32,48},{48,64},{64,80},{80,96},{96,112},{112,128},... | collective-permute-start | bytes 98312 | tf_op jit(solution)/shard_map/while/body/eval_jaxpr/ppermute | solution.py:16
  307.1 6.8 %collective-permute-start = (f32[512,16]{0,1:T(8,128)S(1)}, f32[512,16]{0,1:T(8,128)S(1)}, u32[]{:S(2)}, u32[]{:S(2)}) collective-permute-start(f32[512,16]{0,1:T(8,128)S(1)} %multiply_add_fusion.3), channel_id=1, source_target_pairs={{0,16},{16,32},{32,48},{48,64},{64,80},{80,96},{96,112},{112,128},... | collective-permute-start | bytes 98312 | tf_op jit(solution)/shard_map/while/body/eval_jaxpr/ppermute | solution.py:16
  313.8 6.8 %collective-permute-start = (f32[512,16]{0,1:T(8,128)S(1)}, f32[512,16]{0,1:T(8,128)S(1)}, u32[]{:S(2)}, u32[]{:S(2)}) collective-permute-start(f32[512,16]{0,1:T(8,128)S(1)} %multiply_add_fusion.3), channel_id=1, source_target_pairs={{0,16},{16,32},{32,48},{48,64},{64,80},{80,96},{96,112},{112,128},... | collective-permute-start | bytes 98312 | tf_op jit(solution)/shard_map/while/body/eval_jaxpr/ppermute | solution.py:16
  320.6 6.9 %collective-permute-start = (f32[512,16]{0,1:T(8,128)S(1)}, f32[512,16]{0,1:T(8,128)S(1)}, u32[]{:S(2)}, u32[]{:S(2)}) collective-permute-start(f32[512,16]{0,1:T(8,128)S(1)} %multiply_add_fusion.3), channel_id=1, source_target_pairs={{0,16},{16,32},{32,48},{48,64},{64,80},{80,96},{96,112},{112,128},... | collective-permute-start | bytes 98312 | tf_op jit(solution)/shard_map/while/body/eval_jaxpr/ppermute | solution.py:16
  327.6 6.6 %collective-permute-start = (f32[512,16]{0,1:T(8,128)S(1)}, f32[512,16]{0,1:T(8,128)S(1)}, u32[]{:S(2)}, u32[]{:S(2)}) collective-permute-start(f32[512,16]{0,1:T(8,128)S(1)} %multiply_add_fusion.3), channel_id=1, source_target_pairs={{0,16},{16,32},{32,48},{48,64},{64,80},{80,96},{96,112},{112,128},... | collective-permute-start | bytes 98312 | tf_op jit(solution)/shard_map/while/body/eval_jaxpr/ppermute | solution.py:16
  334.2 6.8 %collective-permute-start = (f32[512,16]{0,1:T(8,128)S(1)}, f32[512,16]{0,1:T(8,128)S(1)}, u32[]{:S(2)}, u32[]{:S(2)}) collective-permute-start(f32[512,16]{0,1:T(8,128)S(1)} %multiply_add_fusion.3), channel_id=1, source_target_pairs={{0,16},{16,32},{32,48},{48,64},{64,80},{80,96},{96,112},{112,128},... | collective-permute-start | bytes 98312 | tf_op jit(solution)/shard_map/while/body/eval_jaxpr/ppermute | solution.py:16
  340.9 6.8 %collective-permute-start = (f32[512,16]{0,1:T(8,128)S(1)}, f32[512,16]{0,1:T(8,128)S(1)}, u32[]{:S(2)}, u32[]{:S(2)}) collective-permute-start(f32[512,16]{0,1:T(8,128)S(1)} %multiply_add_fusion.3), channel_id=1, source_target_pairs={{0,16},{16,32},{32,48},{48,64},{64,80},{80,96},{96,112},{112,128},... | collective-permute-start | bytes 98312 | tf_op jit(solution)/shard_map/while/body/eval_jaxpr/ppermute | solution.py:16
  347.7 4.5 copy-start.4
  347.7 87.2 %copy-start.3 = (f32[4096]{0:T(1024)S(1)}, f32[4096]{0:T(1024)}, u32[]{:S(2)}) copy-start(f32[4096]{0:T(1024)} %param.28) | copy-start | bytes 49156
  352.1 156.4 %all-gather.14.cloned.1.call-start = ((), (), s32[]{:S(2)}) async-start(), calls=%async_computation.9 | async-start | bytes 4456448 | tf_op jit(solution)/shard_map/all_gather | solution.py:137
  455.3 150.4 %reduce-scatter.5.cloned.1.call-start = ((), (), s32[]{:S(2)}) async-start(), calls=%async_computation.10 | async-start | bytes 4456448 | tf_op jit(solution)/shard_map/reduce_scatter | solution.py:146
  607.5 21.1 %all-to-all-start.1 = ((bf16[16,2,4096]{2,1,0:T(2,128)(2,1)}), bf16[16,2,4096]{2,1,0:T(2,128)(2,1)S(1)}, u32[]{:S(2)}, u32[]{:S(2)}) async-start(bf16[16,2,4096]{2,1,0:T(2,128)(2,1)} %reshape.76), calls=%async_computation.3 | async-start | bytes 524288 | tf_op jit(solution)/shard_map/all_to_all | solution.py:149
Sparse Core Ops, SparseCore 0:
  9.1 41.8 all-gather.5
  53.4 55.2 all-gather.7
  111.1 56.2 all-gather.9
  169.7 61.4 all-gather.11
  352.2 81.6 reduce-scatter.2
  455.4 53.0 all-gather.13
  524.8 80.7 reduce-scatter.4
where the time goes:
time: 637 us; the launch traced here: 636 us
  waiting for transfers between devices  394 us (62%)
  starting transfers between devices  87.9 us (14%)
  matrix products  67.4 us (11%)
  blocking collectives  65.7 us (10%)
  between operations  13.7 us (2%)
    reduce_scatter x1, waiting for transfers between devices, local(): lax.psum_scatter(jnp.dot(blender_result, out_whole, preferred_element_typ...  81 us
    reduce_scatter x1, waiting for transfers between devices, local(): lax.psum_scatter(partial_out.astype(jnp.bfloat16), 'ctx', scatter_dimensi...  81 us
    ppermute x16, starting transfers between devices, shifted(): return lax.ppermute(shard, axis, pairs)  78.2 us
    all_gather x1, waiting for transfers between devices, local(): lax.all_gather(input_weight, 'ctx', axis=0, tiled=True)  57.7 us
    all_gather x1, waiting for transfers between devices, local(): shard_rows = lax.all_gather(arrived, 'ctx', axis=0, tiled=True)  53 us
    all_gather x1, waiting for transfers between devices, local(): lax.all_gather(gate_weight, 'ctx', axis=0, tiled=True)  52.4 us
    psum x1, blocking collectives, local(): lax.psum(jnp.dot(mixer_in, state_weight, preferred_element_type=jnp.float...  46.7 us
    all_gather x1, waiting for transfers between devices, local(): whole_stretch = lax.all_gather(tokens, 'exp', axis=1, tiled=True)  39.5 us
  transfers between devices with their start and end apart: 24, of which 22 were waited for; matrix products, arithmetic and copies ran while one was open for 8% of the time, Pallas kernels for 0%

commit v1 on v0

--- a/solution.py
+++ b/solution.py
@@ -1,3 +1,4 @@
+import functools
 import jax
 import jax.numpy as jnp
 from jax import lax
@@ -8,6 +9,31 @@
 TOP = 2
 CAP = 2
 precise = lax.Precision.HIGHEST
+
+
+def close_leaves(xs, d_out):
+    answer = lax.axis_size("ctx")
+    heard = lax.axis_index("ctx")
+    high, block_last, state_next = (answer, heard, xs.shape[d_out])
+    queue = [h * high if idx == d_out else h for idx, h in enumerate(xs.shape)]
+    val2 = lax.dynamic_update_slice_in_dim(
+        jnp.zeros(queue, xs.dtype), xs, block_last * state_next, axis=d_out
+    )
+    formed = last = xs
+    for p in tuple(range(1, high // 2 + 1)):
+        formed = lax.ppermute(formed, "ctx", [(idx, (idx + 1) % high) for idx in range(high)])
+        val2 = lax.dynamic_update_slice_in_dim(
+            val2, formed, (block_last - p) % high * state_next, axis=d_out
+        )
+        if 2 * p < high:
+            last = lax.ppermute(last, "ctx", [(idx, (idx - 1) % high) for idx in range(high)])
+            val2 = lax.dynamic_update_slice_in_dim(
+                val2, last, (block_last + p) % high * state_next, axis=d_out
+            )
+    return val2
+
+
+series_all_try_all = functools.partial(close_leaves, d_out=0)
 
 
 def shifted(shard, axis, by):
@@ -50,9 +76,7 @@
         preferred_element_type=jnp.float32,
     )
     inner_z = jnp.dot(
-        whole_stretch,
-        lax.all_gather(gate_weight, "ctx", axis=0, tiled=True),
-        preferred_element_type=jnp.float32,
+        whole_stretch, series_all_try_all(gate_weight), preferred_element_type=jnp.float32
     )
     inner_x = inner_x.astype(jnp.bfloat16)
     inner_z = inner_z.astype(jnp.bfloat16)

time: 637 us -> 592 us (0.929)
  waiting for transfers between devices: 394 us -> 297 us
  starting transfers between devices: 87.9 us -> 124 us
  local copies, waits for them, and re-layouts: 4.31 us -> 18.1 us
    all_gather x1 -> x0, waiting for transfers between devices: 52.4 us -> none  [local(): lax.all_gather(gate_weight, 'ctx', axis=0, tiled=True)]
    all_gather x1, waiting for transfers between devices: 39.5 us -> 0.01 us  [local(): whole_stretch = lax.all_gather(tokens, 'exp', axis=1, tiled=True)]
    ppermute x0 -> x15, starting transfers between devices: none -> 36 us  [the longest x7 33.8 us: close_leaves(): lax.ppermute(last, 'ctx', [(idx, (idx - 1) % high) for idx in range(high)])]
    all_gather x1, waiting for transfers between devices: 57.7 us -> 26.7 us  [local(): lax.all_gather(input_weight, 'ctx', axis=0, tiled=True)]
    ppermute x0 -> x15, waiting for transfers between devices: none -> 26.4 us  [the longest x8 17 us: close_leaves(): lax.ppermute(formed, 'ctx', [(idx, (idx + 1) % high) for idx in range(hig...]
    dynamic_update_slice x0 -> x16, local copies, waits for them, and re-layouts: none -> 11.6 us  [the longest x8 5.77 us: close_leaves(): lax.dynamic_update_slice_in_dim(val2, formed, (block_last - p) % high * s...]
  transfers between devices with their start and end apart: 24 -> 38, of which waited for: 22 -> 30; matrix products, arithmetic and copies ran while one was open for 8% -> 11% of each run, Pallas kernels for 0% -> 0%
where the time goes in v1:
time: 592 us; the launch traced here: 591 us
  waiting for transfers between devices  297 us (50%)
  starting transfers between devices  124 us (21%)
  matrix products  67.6 us (11%)
  blocking collectives  66.8 us (11%)
  local copies, waits for them, and re-layouts  18.1 us (3%)
  between operations  13.7 us (2%)
    reduce_scatter x1, waiting for transfers between devices, local(): lax.psum_scatter(jnp.dot(blender_result, out_whole, preferred_element_typ...  82.1 us
    reduce_scatter x1, waiting for transfers between devices, local(): lax.psum_scatter(partial_out.astype(jnp.bfloat16), 'ctx', scatter_dimensi...  80.9 us
    ppermute x16, starting transfers between devices, shifted(): return lax.ppermute(shard, axis, pairs)  78.2 us
    all_gather x1, waiting for transfers between devices, local(): shard_rows = lax.all_gather(arrived, 'ctx', axis=0, tiled=True)  52.9 us
    psum x1, blocking collectives, local(): lax.psum(jnp.dot(mixer_in, state_weight, preferred_element_type=jnp.float...  47.4 us
    dot_general x4, matrix products, causal_part(): jnp.einsum('ts,tsc,sc->tc', scores, weight, input_block, precision=precise)  38.7 us
    ppermute x7, starting transfers between devices, close_leaves(): lax.ppermute(last, 'ctx', [(idx, (idx - 1) % high) for idx in range(high)])  33.8 us
    all_gather x1, waiting for transfers between devices, local(): lax.all_gather(input_weight, 'ctx', axis=0, tiled=True)  26.7 us
  transfers between devices with their start and end apart: 38, of which 30 were waited for; matrix products, arithmetic and copies ran while one was open for 11% of the time, Pallas kernels for 0%

profile of v1, /device:TPU:1, one launch (start us, length us, event | category | flops | bytes accessed | tf_op | source)
XLA Modules:
  0.0 590.6 jit_solution(14906479348774006445)
XLA Ops:
  18.2 4.8 collective-permute-start.5
  28.8 4.9 collective-permute-start.7
  47.1 5.2 collective-permute-start.11
  56.1 5.2 collective-permute-start.13
  67.5 5.2 collective-permute-start.15
  80.6 5.0 collective-permute-done.16
  86.4 26.7 %all-gather.7.cloned.1.call-done = bf16[4096,512]{1,0:T(8,128)(2,1)} async-done(((bf16[256,512]{1,0:T(8,128)(2,1)}), bf16[4096,512]{1,0:T(8,128)(2,1)}) %all-gather.7.cloned.1.call-update) | async-done | bytes 4194320 | tf_op jit(solution)/shard_map/all_gather | solution.py:75
  122.8 47.4 %psum.7 = f32[128,32]{0,1:T(8,128)S(1)} all-reduce(f32[128,32]{0,1:T(8,128)S(1)} %fusion.55), channel_id=1, replica_groups=mesh['ctx'=16,'exp'=16] {'exp'}, use_global_device_ids=true, to_apply=%region_1.2 | all-reduce | flops 4096 | bytes 32768 | tf_op jit(solution)/shard_map/psum | solution.py:92
  170.9 39.0 %while.20 = (s32[]{:T(128)}, f32[4,128,128]{2,1,0:T(8,128)S(1)}, f32[4,128,128]{2,1,0:T(8,128)S(1)}, f32[4,128,128]{2,1,0:T(8,128)S(1)}, f32[128,128]{1,0:T(8,128)S(1)}, /*index=5*/s32[]{:T(128)}) while((s32[]{:T(128)}, f32[4,128,128]{2,1,0:T(8,128)S(1)}, f32[4,128,128]{2,1,0:T(8,128)S(1)}, f32[4,128,128]{2,1,0:T(8,128)S(1)}, ...), condition=%wide.region_3.4_spmd, body=%wide.region_2.3_spmd.sunk | while | flops 35667968 | bytes 688205 | solution.py:103
  170.9 9.7 %fusion.88 = f32[128,1,128]{2,1,0:T(1,128)S(1)} fusion(f32[128,128,1]{1,2,0:T(1,128)S(1)} %bitcast.90, f32[128,128]{1,0:T(8,128)S(1)} %get-tuple-element.140, f32[128,128]{1,0:T(8,128)S(1)} %get-tuple-element.141, pred[128,128]{1,0:T(8,128)(4,1)S(1)} %iota_compare_fusion.5), kind=kOutput, calls=%fused_computation.clone.1 | convolution fusion | flops 35651584 | bytes 278528 | tf_op jit(solution)/shard_map/while/body/eval_jaxpr/ts,tsc,sc->tc/dot_general | solution.py:50
  180.7 9.7 %fusion.88 = f32[128,1,128]{2,1,0:T(1,128)S(1)} fusion(f32[128,128,1]{1,2,0:T(1,128)S(1)} %bitcast.90, f32[128,128]{1,0:T(8,128)S(1)} %get-tuple-element.140, f32[128,128]{1,0:T(8,128)S(1)} %get-tuple-element.141, pred[128,128]{1,0:T(8,128)(4,1)S(1)} %iota_compare_fusion.5), kind=kOutput, calls=%fused_computation.clone.1 | convolution fusion | flops 35651584 | bytes 278528 | tf_op jit(solution)/shard_map/while/body/eval_jaxpr/ts,tsc,sc->tc/dot_general | solution.py:50
  190.5 9.7 %fusion.88 = f32[128,1,128]{2,1,0:T(1,128)S(1)} fusion(f32[128,128,1]{1,2,0:T(1,128)S(1)} %bitcast.90, f32[128,128]{1,0:T(8,128)S(1)} %get-tuple-element.140, f32[128,128]{1,0:T(8,128)S(1)} %get-tuple-element.141, pred[128,128]{1,0:T(8,128)(4,1)S(1)} %iota_compare_fusion.5), kind=kOutput, calls=%fused_computation.clone.1 | convolution fusion | flops 35651584 | bytes 278528 | tf_op jit(solution)/shard_map/while/body/eval_jaxpr/ts,tsc,sc->tc/dot_general | solution.py:50
  200.2 9.7 %fusion.88 = f32[128,1,128]{2,1,0:T(1,128)S(1)} fusion(f32[128,128,1]{1,2,0:T(1,128)S(1)} %bitcast.90, f32[128,128]{1,0:T(8,128)S(1)} %get-tuple-element.140, f32[128,128]{1,0:T(8,128)S(1)} %get-tuple-element.141, pred[128,128]{1,0:T(8,128)(4,1)S(1)} %iota_compare_fusion.5), kind=kOutput, calls=%fused_computation.clone.1 | convolution fusion | flops 35651584 | bytes 278528 | tf_op jit(solution)/shard_map/while/body/eval_jaxpr/ts,tsc,sc->tc/dot_general | solution.py:50
  209.9 90.5 %while.21 = (s32[]{:T(128)}, f32[512,16]{0,1:T(8,128)S(1)}, f32[512]{0:T(512)S(1)}, f32[512,16]{0,1:T(8,128)S(1)}, s32[]{:T(128)}) while((s32[]{:T(128)}, f32[512,16]{0,1:T(8,128)S(1)}, f32[512]{0:T(512)S(1)}, f32[512,16]{0,1:T(8,128)S(1)}, s32[]{:T(128)}) %tuple.40), condition=%wide.region_5.6_spmd, body=%wide.region_4.5_spmd.sunk | while | flops 16386 | bytes 231525 | solution.py:116
  231.9 5.8 collective-permute-start
  238.7 5.9 %collective-permute-start = (f32[512,16]{0,1:T(8,128)S(1)}, f32[512,16]{0,1:T(8,128)S(1)}, u32[]{:S(2)}, u32[]{:S(2)}) collective-permute-start(f32[512,16]{0,1:T(8,128)S(1)} %multiply_add_fusion.3), channel_id=1, source_target_pairs={{0,16},{16,32},{32,48},{48,64},{64,80},{80,96},{96,112},{112,128},... | collective-permute-start | bytes 98312 | tf_op jit(solution)/shard_map/while/body/eval_jaxpr/ppermute | solution.py:42
  245.6 6.1 %collective-permute-start = (f32[512,16]{0,1:T(8,128)S(1)}, f32[512,16]{0,1:T(8,128)S(1)}, u32[]{:S(2)}, u32[]{:S(2)}) collective-permute-start(f32[512,16]{0,1:T(8,128)S(1)} %multiply_add_fusion.3), channel_id=1, source_target_pairs={{0,16},{16,32},{32,48},{48,64},{64,80},{80,96},{96,112},{112,128},... | collective-permute-start | bytes 98312 | tf_op jit(solution)/shard_map/while/body/eval_jaxpr/ppermute | solution.py:42
  252.7 5.8 collective-permute-start
  259.5 5.8 collective-permute-start
  266.3 5.8 collective-permute-start
  273.1 5.8 collective-permute-start
  279.9 5.7 collective-permute-start
  286.6 5.8 collective-permute-start
  293.4 6.0 %collective-permute-start = (f32[512,16]{0,1:T(8,128)S(1)}, f32[512,16]{0,1:T(8,128)S(1)}, u32[]{:S(2)}, u32[]{:S(2)}) collective-permute-start(f32[512,16]{0,1:T(8,128)S(1)} %multiply_add_fusion.3), channel_id=1, source_target_pairs={{0,16},{16,32},{32,48},{48,64},{64,80},{80,96},{96,112},{112,128},... | collective-permute-start | bytes 98312 | tf_op jit(solution)/shard_map/while/body/eval_jaxpr/ppermute | solution.py:42
  305.7 82.1 %reduce-scatter.3.cloned.1.call-done = bf16[8,4096]{1,0:T(8,128)(2,1)} async-done(((bf16[128,4096]{1,0:T(8,128)(2,1)}), bf16[8,4096]{1,0:T(8,128)(2,1)}) %reduce-scatter.3.cloned.1.call-update) | async-done | bytes 65552 | tf_op jit(solution)/shard_map/reduce_scatter | solution.py:126
  389.3 19.4 %all_to_all.10 = bf16[16,2,4096]{2,1,0:T(2,128)(2,1)S(1)} all-to-all(bf16[16,2,4096]{2,1,0:T(2,128)(2,1)S(1)} %reshape.74), channel_id=1, replica_groups=mesh['ctx'=16,'exp'=16] {'exp'}, dimensions={0} | all-to-all | bytes 524288 | tf_op jit(solution)/shard_map/all_to_all | solution.py:156
  409.8 52.9 %all-gather.11.cloned.1.call-done = bf16[512,4096]{1,0:T(8,128)(2,1)} async-done(((bf16[32,4096]{1,0:T(8,128)(2,1)}), bf16[512,4096]{1,0:T(8,128)(2,1)}) %all-gather.11.cloned.1.call-update) | async-done | bytes 4194320 | tf_op jit(solution)/shard_map/all_gather | solution.py:161
  462.8 5.4 fusion.18
  468.2 10.8 %convolution_convert_fusion = bf16[512,4096]{1,0:T(8,128)(2,1)} fusion(bf16[1,448,4096]{2,1,0:T(8,128)(2,1)} %param.32, bf16[512,4096]{1,0:T(8,128)(2,1)} %all-gather.11.cloned.1.call-done, bf16[1,448,4096]{2,1,0:T(8,128)(2,1)} %param.31, f32[512,448]{0,1:T(8,128)S(1)} %fusion.18), kind=kOutput, calls=%fused_computation.19 | convolution fusion | flops 3761569792 | bytes 16646144 | tf_op jit(solution)/shard_map/dot_general | solution.py:169
  479.0 80.9 %reduce-scatter.5.cloned.1.call-done = bf16[32,4096]{1,0:T(8,128)(2,1)} async-done(((bf16[512,4096]{1,0:T(8,128)(2,1)}), bf16[32,4096]{1,0:T(8,128)(2,1)}) %reduce-scatter.5.cloned.1.call-update) | async-done | bytes 262160 | tf_op jit(solution)/shard_map/reduce_scatter | solution.py:170
  561.7 9.3 %all-to-all-start.1 = ((bf16[16,2,4096]{2,1,0:T(2,128)(2,1)}), bf16[16,2,4096]{2,1,0:T(2,128)(2,1)S(1)}, u32[]{:S(2)}, u32[]{:S(2)}) async-start(bf16[16,2,4096]{2,1,0:T(2,128)(2,1)} %reshape.76), calls=%async_computation.3 | async-start | bytes 524288 | tf_op jit(solution)/shard_map/all_to_all | solution.py:173
  571.6 11.2 %all-to-all-done.1 = bf16[16,2,4096]{2,1,0:T(2,128)(2,1)S(1)} async-done(((bf16[16,2,4096]{2,1,0:T(2,128)(2,1)}), bf16[16,2,4096]{2,1,0:T(2,128)(2,1)S(1)}, u32[]{:S(2)}, u32[]{:S(2)}) %all-to-all-start.1) | async-done | bytes 262176 | tf_op jit(solution)/shard_map/all_to_all | solution.py:173
  (159 shorter events, 103.1 us)
Async XLA Ops:
  6.5 79.9 %all-gather.5.cloned.1.call-start = ((), (), s32[]{:S(2)}) async-start(), calls=%async_computation.4 | async-start | bytes 1114112 | tf_op jit(solution)/shard_map/all_gather | solution.py:70
  7.3 105.8 %all-gather.7.cloned.1.call-start = ((), (), s32[]{:S(2)}) async-start(), calls=%async_computation.5 | async-start | bytes 4456448 | tf_op jit(solution)/shard_map/all_gather | solution.py:75
  8.0 293.0 %all-gather.9.cloned.1.call-start = ((), (), s32[]{:S(2)}) async-start(), calls=%async_computation.6 | async-start | bytes 4456448 | tf_op jit(solution)/shard_map/all_gather | solution.py:125
  8.1 10.1 %collective-permute-start.2 = (bf16[256,512]{1,0:T(8,128)(2,1)}, bf16[256,512]{1,0:T(8,128)(2,1)S(1)}, u32[]{:S(2)}, u32[]{:S(2)}) collective-permute-start(bf16[256,512]{1,0:T(8,128)(2,1)} %param.21), channel_id=1, source_target_pairs={{0,16},{16,32},{32,48},{48,64},{64,80},{80,96},{96,112},{112,128},... | collective-permute-start | bytes 786440 | tf_op jit(solution)/shard_map/ppermute | solution.py:24
  10.2 8.0 %collective-permute-start.3 = (bf16[256,512]{1,0:T(8,128)(2,1)}, bf16[256,512]{1,0:T(8,128)(2,1)S(1)}, u32[]{:S(2)}, u32[]{:S(2)}) collective-permute-start(bf16[256,512]{1,0:T(8,128)(2,1)} %param.21), channel_id=1, source_target_pairs={{0,240},{16,0},{32,16},{48,32},{64,48},{80,64},{96,80},{112,96},{1... | collective-permute-start | bytes 786440 | tf_op jit(solution)/shard_map/ppermute | solution.py:29
  18.2 8.5 %collective-permute-start.4 = (bf16[256,512]{1,0:T(8,128)(2,1)S(1)}, bf16[256,512]{1,0:T(8,128)(2,1)S(1)}, u32[]{:S(2)}, u32[]{:S(2)}) collective-permute-start(bf16[256,512]{1,0:T(8,128)(2,1)S(1)} %collective-permute-done.2), channel_id=1, source_target_pairs={{0,16},{16,32},{32,48},{48,64},{64,80},{80,96},{96,112},{112,128},... | collective-permute-start | bytes 786440 | tf_op jit(solution)/shard_map/ppermute | solution.py:24
  18.2 10.6 %collective-permute-start.5 = (bf16[256,512]{1,0:T(8,128)(2,1)S(1)}, bf16[256,512]{1,0:T(8,128)(2,1)S(1)}, u32[]{:S(2)}, u32[]{:S(2)}) collective-permute-start(bf16[256,512]{1,0:T(8,128)(2,1)S(1)} %collective-permute-done.3), channel_id=1, source_target_pairs={{0,240},{16,0},{32,16},{48,32},{64,48},{80,64},{96,80},{112,96},{1... | collective-permute-start | bytes 786440 | tf_op jit(solution)/shard_map/ppermute | solution.py:29
  23.0 364.8 %reduce-scatter.3.cloned.1.call-start = ((), (), s32[]{:S(2)}) async-start(), calls=%async_computation.7 | async-start | bytes 1114112 | tf_op jit(solution)/shard_map/reduce_scatter | solution.py:126
  26.7 8.5 %collective-permute-start.6 = (bf16[256,512]{1,0:T(8,128)(2,1)S(1)}, bf16[256,512]{1,0:T(8,128)(2,1)S(1)}, u32[]{:S(2)}, u32[]{:S(2)}) collective-permute-start(bf16[256,512]{1,0:T(8,128)(2,1)S(1)} %collective-permute-done.4), channel_id=1, source_target_pairs={{0,16},{16,32},{32,48},{48,64},{64,80},{80,96},{96,112},{112,128},... | collective-permute-start | bytes 786440 | tf_op jit(solution)/shard_map/ppermute | solution.py:24
  28.8 10.2 %collective-permute-start.7 = (bf16[256,512]{1,0:T(8,128)(2,1)S(1)}, bf16[256,512]{1,0:T(8,128)(2,1)S(1)}, u32[]{:S(2)}, u32[]{:S(2)}) collective-permute-start(bf16[256,512]{1,0:T(8,128)(2,1)S(1)} %collective-permute-done.5), channel_id=1, source_target_pairs={{0,240},{16,0},{32,16},{48,32},{64,48},{80,64},{96,80},{112,96},{1... | collective-permute-start | bytes 786440 | tf_op jit(solution)/shard_map/ppermute | solution.py:29
  35.3 9.2 %collective-permute-start.8 = (bf16[256,512]{1,0:T(8,128)(2,1)S(1)}, bf16[256,512]{1,0:T(8,128)(2,1)S(1)}, u32[]{:S(2)}, u32[]{:S(2)}) collective-permute-start(bf16[256,512]{1,0:T(8,128)(2,1)S(1)} %collective-permute-done.6), channel_id=1, source_target_pairs={{0,16},{16,32},{32,48},{48,64},{64,80},{80,96},{96,112},{112,128},... | collective-permute-start | bytes 786440 | tf_op jit(solution)/shard_map/ppermute | solution.py:24
  39.0 8.1 %collective-permute-start.9 = (bf16[256,512]{1,0:T(8,128)(2,1)S(1)}, bf16[256,512]{1,0:T(8,128)(2,1)S(1)}, u32[]{:S(2)}, u32[]{:S(2)}) collective-permute-start(bf16[256,512]{1,0:T(8,128)(2,1)S(1)} %collective-permute-done.7), channel_id=1, source_target_pairs={{0,240},{16,0},{32,16},{48,32},{64,48},{80,64},{96,80},{112,96},{1... | collective-permute-start | bytes 786440 | tf_op jit(solution)/shard_map/ppermute | solution.py:29
  44.5 8.5 %collective-permute-start.10 = (bf16[256,512]{1,0:T(8,128)(2,1)S(1)}, bf16[256,512]{1,0:T(8,128)(2,1)S(1)}, u32[]{:S(2)}, u32[]{:S(2)}) collective-permute-start(bf16[256,512]{1,0:T(8,128)(2,1)S(1)} %collective-permute-done.8), channel_id=1, source_target_pairs={{0,16},{16,32},{32,48},{48,64},{64,80},{80,96},{96,112},{112,128},... | collective-permute-start | bytes 786440 | tf_op jit(solution)/shard_map/ppermute | solution.py:24
  47.1 9.0 %collective-permute-start.11 = (bf16[256,512]{1,0:T(8,128)(2,1)S(1)}, bf16[256,512]{1,0:T(8,128)(2,1)S(1)}, u32[]{:S(2)}, u32[]{:S(2)}) collective-permute-start(bf16[256,512]{1,0:T(8,128)(2,1)S(1)} %collective-permute-done.9), channel_id=1, source_target_pairs={{0,240},{16,0},{32,16},{48,32},{64,48},{80,64},{96,80},{112,96},{1... | collective-permute-start | bytes 786440 | tf_op jit(solution)/shard_map/ppermute | solution.py:29
  53.0 9.3 %collective-permute-start.12 = (bf16[256,512]{1,0:T(8,128)(2,1)S(1)}, bf16[256,512]{1,0:T(8,128)(2,1)S(1)}, u32[]{:S(2)}, u32[]{:S(2)}) collective-permute-start(bf16[256,512]{1,0:T(8,128)(2,1)S(1)} %collective-permute-done.10), channel_id=1, source_target_pairs={{0,16},{16,32},{32,48},{48,64},{64,80},{80,96},{96,112},{112,128},... | collective-permute-start | bytes 786440 | tf_op jit(solution)/shard_map/ppermute | solution.py:24
  56.1 11.4 %collective-permute-start.13 = (bf16[256,512]{1,0:T(8,128)(2,1)S(1)}, bf16[256,512]{1,0:T(8,128)(2,1)S(1)}, u32[]{:S(2)}, u32[]{:S(2)}) collective-permute-start(bf16[256,512]{1,0:T(8,128)(2,1)S(1)} %collective-permute-done.11), channel_id=1, source_target_pairs={{0,240},{16,0},{32,16},{48,32},{64,48},{80,64},{96,80},{112,96},{1... | collective-permute-start | bytes 786440 | tf_op jit(solution)/shard_map/ppermute | solution.py:29
  62.4 13.1 %collective-permute-start.14 = (bf16[256,512]{1,0:T(8,128)(2,1)S(1)}, bf16[256,512]{1,0:T(8,128)(2,1)S(1)}, u32[]{:S(2)}, u32[]{:S(2)}) collective-permute-start(bf16[256,512]{1,0:T(8,128)(2,1)S(1)} %collective-permute-done.12), channel_id=1, source_target_pairs={{0,16},{16,32},{32,48},{48,64},{64,80},{80,96},{96,112},{112,128},... | collective-permute-start | bytes 786440 | tf_op jit(solution)/shard_map/ppermute | solution.py:24
  67.5 12.4 %collective-permute-start.15 = (bf16[256,512]{1,0:T(8,128)(2,1)S(1)}, bf16[256,512]{1,0:T(8,128)(2,1)S(1)}, u32[]{:S(2)}, u32[]{:S(2)}) collective-permute-start(bf16[256,512]{1,0:T(8,128)(2,1)S(1)} %collective-permute-done.13), channel_id=1, source_target_pairs={{0,240},{16,0},{32,16},{48,32},{64,48},{80,64},{96,80},{112,96},{1... | collective-permute-start | bytes 786440 | tf_op jit(solution)/shard_map/ppermute | solution.py:29
  75.5 10.2 %collective-permute-start.16 = (bf16[256,512]{1,0:T(8,128)(2,1)S(1)}, bf16[256,512]{1,0:T(8,128)(2,1)S(1)}, u32[]{:S(2)}, u32[]{:S(2)}) collective-permute-start(bf16[256,512]{1,0:T(8,128)(2,1)S(1)} %collective-permute-done.14), channel_id=1, source_target_pairs={{0,16},{16,32},{32,48},{48,64},{64,80},{80,96},{96,112},{112,128},... | collective-permute-start | bytes 786440 | tf_op jit(solution)/shard_map/ppermute | solution.py:24
  231.9 6.8 %collective-permute-start = (f32[512,16]{0,1:T(8,128)S(1)}, f32[512,16]{0,1:T(8,128)S(1)}, u32[]{:S(2)}, u32[]{:S(2)}) collective-permute-start(f32[512,16]{0,1:T(8,128)S(1)} %multiply_add_fusion.3), channel_id=1, source_target_pairs={{0,16},{16,32},{32,48},{48,64},{64,80},{80,96},{96,112},{112,128},... | collective-permute-start | bytes 98312 | tf_op jit(solution)/shard_map/while/body/eval_jaxpr/ppermute | solution.py:42
  238.7 6.9 %collective-permute-start = (f32[512,16]{0,1:T(8,128)S(1)}, f32[512,16]{0,1:T(8,128)S(1)}, u32[]{:S(2)}, u32[]{:S(2)}) collective-permute-start(f32[512,16]{0,1:T(8,128)S(1)} %multiply_add_fusion.3), channel_id=1, source_target_pairs={{0,16},{16,32},{32,48},{48,64},{64,80},{80,96},{96,112},{112,128},... | collective-permute-start | bytes 98312 | tf_op jit(solution)/shard_map/while/body/eval_jaxpr/ppermute | solution.py:42
  245.6 7.1 %collective-permute-start = (f32[512,16]{0,1:T(8,128)S(1)}, f32[512,16]{0,1:T(8,128)S(1)}, u32[]{:S(2)}, u32[]{:S(2)}) collective-permute-start(f32[512,16]{0,1:T(8,128)S(1)} %multiply_add_fusion.3), channel_id=1, source_target_pairs={{0,16},{16,32},{32,48},{48,64},{64,80},{80,96},{96,112},{112,128},... | collective-permute-start | bytes 98312 | tf_op jit(solution)/shard_map/while/body/eval_jaxpr/ppermute | solution.py:42
  252.7 6.8 %collective-permute-start = (f32[512,16]{0,1:T(8,128)S(1)}, f32[512,16]{0,1:T(8,128)S(1)}, u32[]{:S(2)}, u32[]{:S(2)}) collective-permute-start(f32[512,16]{0,1:T(8,128)S(1)} %multiply_add_fusion.3), channel_id=1, source_target_pairs={{0,16},{16,32},{32,48},{48,64},{64,80},{80,96},{96,112},{112,128},... | collective-permute-start | bytes 98312 | tf_op jit(solution)/shard_map/while/body/eval_jaxpr/ppermute | solution.py:42
  259.5 6.8 %collective-permute-start = (f32[512,16]{0,1:T(8,128)S(1)}, f32[512,16]{0,1:T(8,128)S(1)}, u32[]{:S(2)}, u32[]{:S(2)}) collective-permute-start(f32[512,16]{0,1:T(8,128)S(1)} %multiply_add_fusion.3), channel_id=1, source_target_pairs={{0,16},{16,32},{32,48},{48,64},{64,80},{80,96},{96,112},{112,128},... | collective-permute-start | bytes 98312 | tf_op jit(solution)/shard_map/while/body/eval_jaxpr/ppermute | solution.py:42
  266.3 6.8 %collective-permute-start = (f32[512,16]{0,1:T(8,128)S(1)}, f32[512,16]{0,1:T(8,128)S(1)}, u32[]{:S(2)}, u32[]{:S(2)}) collective-permute-start(f32[512,16]{0,1:T(8,128)S(1)} %multiply_add_fusion.3), channel_id=1, source_target_pairs={{0,16},{16,32},{32,48},{48,64},{64,80},{80,96},{96,112},{112,128},... | collective-permute-start | bytes 98312 | tf_op jit(solution)/shard_map/while/body/eval_jaxpr/ppermute | solution.py:42
  273.1 6.9 %collective-permute-start = (f32[512,16]{0,1:T(8,128)S(1)}, f32[512,16]{0,1:T(8,128)S(1)}, u32[]{:S(2)}, u32[]{:S(2)}) collective-permute-start(f32[512,16]{0,1:T(8,128)S(1)} %multiply_add_fusion.3), channel_id=1, source_target_pairs={{0,16},{16,32},{32,48},{48,64},{64,80},{80,96},{96,112},{112,128},... | collective-permute-start | bytes 98312 | tf_op jit(solution)/shard_map/while/body/eval_jaxpr/ppermute | solution.py:42
  279.9 6.7 %collective-permute-start = (f32[512,16]{0,1:T(8,128)S(1)}, f32[512,16]{0,1:T(8,128)S(1)}, u32[]{:S(2)}, u32[]{:S(2)}) collective-permute-start(f32[512,16]{0,1:T(8,128)S(1)} %multiply_add_fusion.3), channel_id=1, source_target_pairs={{0,16},{16,32},{32,48},{48,64},{64,80},{80,96},{96,112},{112,128},... | collective-permute-start | bytes 98312 | tf_op jit(solution)/shard_map/while/body/eval_jaxpr/ppermute | solution.py:42
  286.6 6.8 %collective-permute-start = (f32[512,16]{0,1:T(8,128)S(1)}, f32[512,16]{0,1:T(8,128)S(1)}, u32[]{:S(2)}, u32[]{:S(2)}) collective-permute-start(f32[512,16]{0,1:T(8,128)S(1)} %multiply_add_fusion.3), channel_id=1, source_target_pairs={{0,16},{16,32},{32,48},{48,64},{64,80},{80,96},{96,112},{112,128},... | collective-permute-start | bytes 98312 | tf_op jit(solution)/shard_map/while/body/eval_jaxpr/ppermute | solution.py:42
  293.4 7.1 %collective-permute-start = (f32[512,16]{0,1:T(8,128)S(1)}, f32[512,16]{0,1:T(8,128)S(1)}, u32[]{:S(2)}, u32[]{:S(2)}) collective-permute-start(f32[512,16]{0,1:T(8,128)S(1)} %multiply_add_fusion.3), channel_id=1, source_target_pairs={{0,16},{16,32},{32,48},{48,64},{64,80},{80,96},{96,112},{112,128},... | collective-permute-start | bytes 98312 | tf_op jit(solution)/shard_map/while/body/eval_jaxpr/ppermute | solution.py:42
  305.0 157.8 %all-gather.11.cloned.1.call-start = ((), (), s32[]{:S(2)}) async-start(), calls=%async_computation.8 | async-start | bytes 4456448 | tf_op jit(solution)/shard_map/all_gather | solution.py:161
  409.5 150.3 %reduce-scatter.5.cloned.1.call-start = ((), (), s32[]{:S(2)}) async-start(), calls=%async_computation.9 | async-start | bytes 4456448 | tf_op jit(solution)/shard_map/reduce_scatter | solution.py:170
  561.7 21.1 %all-to-all-start.1 = ((bf16[16,2,4096]{2,1,0:T(2,128)(2,1)}), bf16[16,2,4096]{2,1,0:T(2,128)(2,1)S(1)}, u32[]{:S(2)}, u32[]{:S(2)}) async-start(bf16[16,2,4096]{2,1,0:T(2,128)(2,1)} %reshape.76), calls=%async_computation.3 | async-start | bytes 524288 | tf_op jit(solution)/shard_map/all_to_all | solution.py:173
  (14 other events, 891.7 us)
Sparse Core Ops, SparseCore 0:
  9.1 41.7 all-gather.4
  53.4 59.6 all-gather.6
  115.5 61.4 all-gather.8
  305.1 82.7 reduce-scatter.2
  409.7 53.0 all-gather.10
  479.1 80.7 reduce-scatter.4
